TPU v7x, 512 devices: a whole 4x8x8 slice. The times are simulated.
512 devices in a mesh: aa: 8 (over x, core), ba: 8 (over y), col: 8 (over z).
Axes of the slice: x: 4, y: 8, z: 8, core: 2. Of those that a mesh axis runs over, the one named last changes fastest.
Arguments:
- field: float32 [192, 1024, 1024], P('col', 'aa', 'ba'), may hold values from -6 to 6
- factor: float32 [1024, 256], P('aa'), may hold values from -0.1875 to 0.1875
Outputs:
- gram: float32 [1024, 1024], P('ba', ('aa', 'col'))
All inputs are finite; a program needn't handle non-finite values.
Results may differ from a plain program's by a relative error of at most 0.000076.
Values sent between devices are 32-bit elements; how exact they have to be, the bound alone decides.
A program may use at most 64 MiB of HBM per device.

v0:
```python
import jax
import jax.numpy as jnp
from jax import lax
from jax.sharding import PartitionSpec as P


def shards(field, factor):
    ranks = factor.shape[1]
    depth = field.shape[0] * lax.axis_size("col")
    partial_core = jnp.einsum("kab,ar->krb", field, factor, precision=lax.Precision.HIGHEST)
    core = lax.psum_scatter(partial_core, "aa", scatter_dimension=1, tiled=True)
    block = jnp.einsum(
        "krb,krc->bc",
        core,
        lax.all_gather(core, "ba", axis=2, tiled=True),
        precision=lax.Precision.HIGHEST,
    )
    summed = lax.psum_scatter(block, ("aa", "col"), scatter_dimension=1, tiled=True)
    return summed / jnp.sqrt(jnp.float32(ranks * depth))


def solution(mesh):
    placed = (P("col", "aa", "ba"), P("aa", None))
    return jax.shard_map(
        shards, mesh=mesh, in_specs=placed, out_specs=P("ba", ("aa", "col")), check_vma=False
    )
```

profile of v0, /device:TPU:8, one launch (start us, length us, event | category | flops | bytes accessed | tf_op | source)
XLA Modules:
  0.0 328.2 jit_solution(14949219071277259198)
XLA Ops:
  6.5 0.0 copy-start
  6.5 0.0 reduce-scatter.2.cloned.1.call-start
  6.5 1.4 copy-done
  7.9 5.2 %convolution_bitcast_fusion = f32[24,256,128]{2,1,0:T(8,128)} fusion(f32[24,128,128]{2,1,0:T(8,128)S(1)} %copy-done, f32[128,256]{1,0:T(8,128)} %param.3), kind=kOutput, calls=%fused_computation | convolution fusion | flops 1207959552 | bytes 4849664 | tf_op jit(solution)/shard_map/kab,ar->krb/dot_general | solution.py:10
  13.2 0.0 reduce-scatter.2.cloned.1.call-update
  13.2 0.0 all-gather.2.cloned.1.call-start
  13.2 45.9 %reduce-scatter.2.cloned.1.call-done = f32[24,32,128]{2,1,0:T(8,128)} async-done(((f32[24,256,128]{2,1,0:T(8,128)}), f32[24,32,128]{2,1,0:T(8,128)}) %reduce-scatter.2.cloned.1.call-update) | async-done | bytes 393232 | tf_op jit(solution)/shard_map/reduce_scatter | solution.py:11
  59.1 0.0 all-gather.2.cloned.1.call-update
  59.2 0.0 all-reduce.3.cloned.1.call-start
  59.2 59.3 %all-gather.2.cloned.1.call-done = f32[24,32,1024]{2,1,0:T(8,128)} async-done(((f32[24,32,128]{2,1,0:T(8,128)}), f32[24,32,1024]{2,1,0:T(8,128)}) %all-gather.2.cloned.1.call-update) | async-done | bytes 3145744 | tf_op jit(solution)/shard_map/all_gather | solution.py:15
  118.5 7.9 %convolution_bitcast_fusion.1 = f32[128,1024]{0,1:T(8,128)} fusion(f32[24,32,128]{2,1,0:T(8,128)} %reduce-scatter.2.cloned.1.call-done, f32[24,32,1024]{2,1,0:T(8,128)} %all-gather.2.cloned.1.call-done), kind=kOutput, calls=%fused_computation.1 | convolution fusion | flops 1207959552 | bytes 4063232 | tf_op jit(solution)/shard_map/krb,krc->bc/dot_general | solution.py:12
  126.4 0.0 all-reduce.3.cloned.1.call-update
  126.4 1.3 dynamic-slice
  128.3 192.1 %all-reduce.3.cloned.1.call-done = f32[128,1024]{0,1:T(8,128)} async-done(((f32[128,1024]{0,1:T(8,128)}), f32[128,1024]{0,1:T(8,128)}) %all-reduce.3.cloned.1.call-update) | async-done | bytes 524304
  320.4 1.3 dynamic-slice_multiply_fusion
Async XLA Ops:
  6.5 1.4 copy-start
  6.5 52.6 %reduce-scatter.2.cloned.1.call-start = ((), (), s32[]{:S(2)}) async-start(), calls=%async_computation.1 | async-start | bytes 3538944 | tf_op jit(solution)/shard_map/reduce_scatter | solution.py:11
  13.2 105.3 %all-gather.2.cloned.1.call-start = ((), (), s32[]{:S(2)}) async-start(), calls=%async_computation.2 | async-start | bytes 3538944 | tf_op jit(solution)/shard_map/all_gather | solution.py:15
  59.2 261.2 %all-reduce.3.cloned.1.call-start = ((), (), s32[]{:S(2)}) async-start(), calls=%async_computation.3 | async-start | bytes 1048576
Sparse Core Ops, SparseCore 0:
  13.3 45.7 reduce-scatter.1
  61.1 57.3 all-gather.1
  126.5 193.8 all-reduce.2
where the time goes:
time: 328 us
  waiting for transfers between devices  297 us (91%)
  between operations  13.8 us (4%)
  matrix products  13.1 us (4%)
    unnamed x4, waiting for transfers between devices  192 us
    all_gather x1, waiting for transfers between devices, shards(): lax.all_gather(core, 'ba', axis=2, tiled=True)  59.3 us
    reduce_scatter x1, waiting for transfers between devices, shards(): core = lax.psum_scatter(partial_core, 'aa', scatter_dimension=1, tiled=True)  45.9 us
    dot_general x1, matrix products, shards(): jnp.einsum('krb,krc->bc', core, lax.all_gather(core, 'ba', axis=2, tiled=...  7.85 us
  transfers between devices with their start and end apart: 3, of which 3 were waited for; matrix products, arithmetic and copies ran while one was open for 0% of the time, Pallas kernels for 0%

commit v1 on v0

--- a/solution.py
+++ b/solution.py
@@ -2,6 +2,13 @@
 import jax.numpy as jnp
 from jax import lax
 from jax.sharding import PartitionSpec as P
+
+
+def exchange_gather(x, axis, along):
+    size = lax.axis_size(axis)
+    parts = jnp.stack([x for _ in range(size)])
+    parts = lax.all_to_all(parts, axis, split_axis=0, concat_axis=0)
+    return jnp.concatenate(parts, axis=along)
 
 
 def shards(field, factor):
@@ -10,10 +17,7 @@
     partial_core = jnp.einsum("kab,ar->krb", field, factor, precision=lax.Precision.HIGHEST)
     core = lax.psum_scatter(partial_core, "aa", scatter_dimension=1, tiled=True)
     block = jnp.einsum(
-        "krb,krc->bc",
-        core,
-        lax.all_gather(core, "ba", axis=2, tiled=True),
-        precision=lax.Precision.HIGHEST,
+        "krb,krc->bc", core, exchange_gather(core, "ba", 2), precision=lax.Precision.HIGHEST
     )
     summed = lax.psum_scatter(block, ("aa", "col"), scatter_dimension=1, tiled=True)
     return summed / jnp.sqrt(jnp.float32(ranks * depth))

time: 328 us -> 345 us (1.052)
  blocking collectives: 0 us -> 76.6 us
  waiting for transfers between devices: 297 us -> 237 us
    all_to_all x0 -> x1, blocking collectives: none -> 76.6 us  [exchange_gather(): parts = lax.all_to_all(parts, axis, split_axis=0, concat_axis=0)]
    all_gather x1 -> x0, waiting for transfers between devices: 59.3 us -> none  [shards(): lax.all_gather(core, 'ba', axis=2, tiled=True)]
    unnamed x4 -> x3, waiting for transfers between devices: 192 us -> 191 us
  transfers between devices with their start and end apart: 3 -> 2, of which waited for: 3 -> 2; matrix products, arithmetic and copies ran while one was open for 0% -> 0% of each run, Pallas kernels for 0% -> 0%
where the time goes in v1:
time: 345 us
  waiting for transfers between devices  237 us (69%)
  blocking collectives  76.6 us (22%)
  between operations  14.1 us (4%)
  matrix products  11.2 us (3%)
  local copies, waits for them, and re-layouts  4.07 us (1%)
    unnamed x3, waiting for transfers between devices  191 us
    all_to_all x1, blocking collectives, exchange_gather(): parts = lax.all_to_all(parts, axis, split_axis=0, concat_axis=0)  76.6 us
    reduce_scatter x1, waiting for transfers between devices, shards(): core = lax.psum_scatter(partial_core, 'aa', scatter_dimension=1, tiled=True)  45.9 us
  transfers between devices with their start and end apart: 2, of which 2 were waited for; matrix products, arithmetic and copies ran while one was open for 0% of the time, Pallas kernels for 0%

profile of v1, /device:TPU:8, one launch (start us, length us, event | category | flops | bytes accessed | tf_op | source)
XLA Modules:
  0.0 344.5 jit_solution(8758493183253980953)
XLA Ops:
  6.5 0.0 copy-start
  6.5 0.0 reduce-scatter.2.cloned.1.call-start
  6.5 1.4 copy-done
  7.9 5.2 %convolution_bitcast_fusion = f32[24,256,128]{2,1,0:T(8,128)} fusion(f32[24,128,128]{2,1,0:T(8,128)S(1)} %copy-done, f32[128,256]{1,0:T(8,128)} %param.3), kind=kOutput, calls=%fused_computation.3 | convolution fusion | flops 1207959552 | bytes 4849664 | tf_op jit(solution)/shard_map/kab,ar->krb/dot_general | solution.py:17
  13.2 0.0 reduce-scatter.2.cloned.1.call-update
  13.2 0.0 all-reduce.3.cloned.1.call-start
  13.2 45.9 %reduce-scatter.2.cloned.1.call-done = f32[24,32,128]{2,1,0:T(8,128)} async-done(((f32[24,256,128]{2,1,0:T(8,128)}), f32[24,32,128]{2,1,0:T(8,128)}) %reduce-scatter.2.cloned.1.call-update) | async-done | bytes 393232 | tf_op jit(solution)/shard_map/reduce_scatter | solution.py:18
  59.2 1.4 stack.2
  60.5 0.0 copy-start.1
  60.6 76.6 %all_to_all.5 = f32[8,24,32,128]{3,2,1,0:T(8,128)S(1)} all-to-all(f32[8,24,32,128]{3,2,1,0:T(8,128)S(1)} %stack.2), channel_id=1, replica_groups=mesh['aa'=8,'ba'=8,'col'=8] {'ba'}, dimensions={0} | all-to-all | bytes 6291456 | tf_op jit(solution)/shard_map/all_to_all | solution.py:10
  137.2 0.0 copy-done.1
  137.2 6.0 %fusion.3 = f32[128,1024]{0,1:T(8,128)} fusion(f32[24,32,128]{2,1,0:T(8,128)S(1)} %copy-done.1, f32[8,24,32,128]{3,2,1,0:T(8,128)S(1)} %all_to_all.5), kind=kOutput, calls=%fused_computation.4 | convolution fusion | flops 1207959552 | bytes 4063232 | tf_op jit(solution)/shard_map/krb,krc->bc/dot_general | solution.py:19
  143.1 0.0 all-reduce.3.cloned.1.call-update
  143.2 1.3 dynamic-slice
  145.1 191.3 %all-reduce.3.cloned.1.call-done = f32[128,1024]{0,1:T(8,128)} async-done(((f32[128,1024]{0,1:T(8,128)}), f32[128,1024]{0,1:T(8,128)}) %all-reduce.3.cloned.1.call-update) | async-done | bytes 524304
  336.4 1.3 dynamic-slice_multiply_fusion
Async XLA Ops:
  6.5 1.4 copy-start
  6.5 52.6 %reduce-scatter.2.cloned.1.call-start = ((), (), s32[]{:S(2)}) async-start(), calls=%async_computation.2 | async-start | bytes 3538944 | tf_op jit(solution)/shard_map/reduce_scatter | solution.py:18
  13.2 323.2 %all-reduce.3.cloned.1.call-start = ((), (), s32[]{:S(2)}) async-start(), calls=%async_computation.3 | async-start | bytes 1048576
  60.5 76.6 %copy-start.1 = (f32[24,32,128]{2,1,0:T(8,128)S(1)}, f32[24,32,128]{2,1,0:T(8,128)}, u32[]{:S(2)}) copy-start(f32[24,32,128]{2,1,0:T(8,128)} %reduce-scatter.2.cloned.1.call-done) | copy-start | bytes 1179652
Sparse Core Ops, SparseCore 0:
  13.3 45.7 reduce-scatter.1
  143.3 193.0 all-reduce.2
